TPU v7x, 32 devices: a whole 2x2x4 slice. The times are simulated.
32 devices in a mesh: dp: 8 (over y, x, core), tensor: 4 (over z).
Axes of the slice: x: 2, y: 2, z: 4, core: 2. Of those that a mesh axis runs over, the one named last changes fastest.
Arguments:
- inputs: bfloat16 [8, 1024, 768], P('dp', 'tensor'), may hold values from -6 to 6
- ln_gain: float32 [768], P(('dp', 'tensor')), may hold values from 0.25 to 1.75
- ln_bias: float32 [768], P(('dp', 'tensor')), may hold values from -1.5 to 1.5
- w_qkv: bfloat16 [768, 3, 768], P('dp', None, 'tensor'), may hold values from -1.5 to 1.5, as said below
- b_qkv: bfloat16 [3, 12, 64], P(None, 'tensor', 'dp'), may hold values from -2.5 to 2.5
- w_out: bfloat16 [768, 768], P('tensor', 'dp'), may hold values from -0.875 to 0.875
- w_in: bfloat16 [768, 3072], P('dp', 'tensor'), may hold values from -0.21875 to 0.21875
- b_in: bfloat16 [24, 128], P('tensor', 'dp'), may hold values from -2.5 to 2.5
- w_down: bfloat16 [3072, 768], P('tensor', 'dp'), may hold values from -0.109375 to 0.109375
- out_bias: float32 [2, 768], P(None, ('dp', 'tensor')), may hold values from -2.5 to 2.5
- cotangent: bfloat16 [8, 1024, 768], P('dp', 'tensor'), may hold values from -6 to 6
Outputs:
- outputs: bfloat16 [8, 1024, 768], P('dp', 'tensor')
- input_grad: bfloat16 [8, 1024, 768], P('dp', 'tensor')
- ln_gain_grad: float32 [768], P(('dp', 'tensor'))
- ln_bias_grad: float32 [768], P(('dp', 'tensor'))
- w_qkv_grad: float32 [768, 3, 768], P('dp', None, 'tensor')
- b_qkv_grad: float32 [3, 12, 64], P(None, 'tensor', 'dp')
- w_out_grad: float32 [768, 768], P('tensor', 'dp')
- w_in_grad: float32 [768, 3072], P('dp', 'tensor')
- b_in_grad: float32 [24, 128], P('tensor', 'dp')
- w_down_grad: float32 [3072, 768], P('tensor', 'dp')
- out_bias_grad: float32 [2, 768], P(None, ('dp', 'tensor'))
Inputs may be any that keep to these rules, and one draw needn't show every extreme that they name: `w_qkv`: projection weights of the queries, keys and values.
All inputs are finite; a program needn't handle non-finite values.
Results may differ from a plain program's by a relative error of at most 0.0082.
Values may be sent and summed in bfloat16 or wider, within the bound.
No kernel may reach another device: no remote copies, remote signals or barrier semaphores. Data moves between devices by JAX's collectives and lax.ppermute only.
A program may use at most 128 MiB of HBM per device.

v0:
```python
import math
import jax
import jax.numpy as jnp
from jax import lax
from jax.sharding import PartitionSpec as P

ROT = 16
EPS = 1e-05
ROOT_HALF = 0.7071067811865476
INV_ROOT_TAU = 0.3989422804014327
NEG_BIG = -1e30


def rotary_tables(length, rot_dims):
    half_rot = rot_dims // 2
    position = jnp.arange(length).astype(jnp.float32)
    inv_freq = jnp.exp(
        jnp.arange(half_rot).astype(jnp.float32) * (-2.0 * math.log(10000.0) / rot_dims)
    )
    angles = position[:, None] * inv_freq[None, :]
    return (jnp.cos(angles), jnp.sin(angles))


def rotate(tensor_in, cosine_table, sine_table, rot_dims, direction):
    half_rot = rot_dims // 2
    first_half = tensor_in[..., :half_rot]
    second_half = tensor_in[..., half_rot:rot_dims]
    cos_rows = cosine_table[:, None, :]
    sin_rows = sine_table[:, None, :] * direction
    return jnp.concatenate(
        [
            first_half * cos_rows - second_half * sin_rows,
            second_half * cos_rows + first_half * sin_rows,
            tensor_in[..., rot_dims:],
        ],
        axis=-1,
    )


def gelu_parts(pre_act):
    normal_cdf = 0.5 * (1.0 + lax.erf(pre_act * ROOT_HALF))
    normal_pdf = jnp.exp(-0.5 * pre_act * pre_act) * INV_ROOT_TAU
    return (pre_act * normal_cdf, normal_cdf + pre_act * normal_pdf)


def masked_scores(q_rows, key_rows, first_row, block_rows, length):
    head_dim = q_rows.shape[-1]
    scores = jnp.einsum(
        "qhd,khd->hqk", q_rows, key_rows, preferred_element_type=jnp.float32
    ) / math.sqrt(head_dim)
    key_pos = jnp.arange(length)
    allowed = (first_row + jnp.arange(block_rows))[:, None] >= key_pos[None, :]
    return jnp.where(allowed[None], scores, NEG_BIG)


def attend(triple):
    queries, key_rows, value_rows = triple
    length = queries.shape[0]
    block_rows = min(512, length)

    def one_block(first_row):
        q_rows = lax.dynamic_slice_in_dim(queries, first_row, block_rows, 0)
        scores = masked_scores(q_rows, key_rows, first_row, block_rows, length)
        row_max = jnp.max(scores, axis=-1, keepdims=True)
        exponent = jnp.exp(scores - row_max)
        row_total = jnp.sum(exponent, axis=-1, keepdims=True)
        attn_probs = (exponent / row_total).astype(jnp.bfloat16)
        context = jnp.einsum(
            "hqk,khd->qhd", attn_probs, value_rows, preferred_element_type=jnp.float32
        )
        return (context.astype(jnp.bfloat16), (row_max + jnp.log(row_total))[..., 0])

    starts = jnp.arange(length // block_rows) * block_rows
    context, logsum = lax.map(one_block, starts)
    return (context.reshape(queries.shape), logsum)


def attend_back(group):
    queries, key_rows, value_rows, logsum, ctx_grad = group
    length = queries.shape[0]
    block_rows = min(512, length)
    head_dim = queries.shape[-1]

    def one_block(carry, block_index):
        key_grad, value_grad = carry
        first_row = block_index * block_rows
        q_rows = lax.dynamic_slice_in_dim(queries, first_row, block_rows, 0)
        d_rows = lax.dynamic_slice_in_dim(ctx_grad, first_row, block_rows, 0)
        scores = masked_scores(q_rows, key_rows, first_row, block_rows, length)
        attn_probs = jnp.exp(scores - logsum[block_index][..., None])
        value_grad = value_grad + jnp.einsum(
            "hqk,qhd->khd",
            attn_probs.astype(jnp.bfloat16),
            d_rows,
            preferred_element_type=jnp.float32,
        )
        prob_grad = jnp.einsum(
            "qhd,khd->hqk", d_rows, value_rows, preferred_element_type=jnp.float32
        )
        row_dot = jnp.sum(attn_probs * prob_grad, axis=-1, keepdims=True)
        score_grad = (attn_probs * (prob_grad - row_dot) / math.sqrt(head_dim)).astype(jnp.bfloat16)
        query_grad = jnp.einsum(
            "hqk,khd->qhd", score_grad, key_rows, preferred_element_type=jnp.float32
        )
        key_grad = key_grad + jnp.einsum(
            "hqk,qhd->khd", score_grad, q_rows, preferred_element_type=jnp.float32
        )
        return ((key_grad, value_grad), query_grad)

    zero_grads = jnp.zeros(queries.shape, jnp.float32)
    (key_grad, value_grad), query_grad = lax.scan(
        one_block, (zero_grads, zero_grads), jnp.arange(length // block_rows)
    )
    return (query_grad.reshape(queries.shape), key_grad, value_grad)


def body(inputs, ln_gain, ln_bias, w_qkv, b_qkv, w_out, w_in, b_in, w_down, out_bias, cotangent):
    gain, shift, biases = (
        lax.all_gather(ln_gain, ("dp", "tensor"), axis=0, tiled=True),
        lax.all_gather(ln_bias, ("dp", "tensor"), axis=0, tiled=True),
        lax.all_gather(out_bias, ("dp", "tensor"), axis=1, tiled=True),
    )
    forward_weights = (
        lax.all_gather(w_qkv, "dp", axis=0, tiled=True),
        lax.all_gather(b_qkv, "dp", axis=2, tiled=True),
        lax.all_gather(w_out, "dp", axis=1, tiled=True),
        lax.all_gather(w_in, "dp", axis=0, tiled=True),
        lax.all_gather(b_in, "dp", axis=1, tiled=True),
        lax.all_gather(w_down, "dp", axis=1, tiled=True),
    )
    qkv_full, qkv_bias, out_full, in_full, in_bias, down_full = forward_weights
    model = qkv_full.shape[0]
    heads = qkv_bias.shape[1]
    head_dim = qkv_bias.shape[2]
    local_width = heads * head_dim
    hidden_units = in_full.shape[1]
    input_full = inputs.astype(jnp.float32)
    centred = input_full - jnp.mean(input_full, axis=-1, keepdims=True)
    inv_sigma = lax.rsqrt(jnp.mean(centred * centred, axis=-1, keepdims=True) + EPS)
    unit_rows = centred * inv_sigma
    normed = (unit_rows * gain + shift).astype(jnp.bfloat16)
    gathered = lax.all_gather(normed, "tensor", axis=1, tiled=True)
    seqs = gathered.shape[0]
    length = gathered.shape[1]
    total_rows = seqs * length
    flat_normed = gathered.reshape(total_rows, model)
    qkv_matrix = qkv_full.reshape(model, 3 * local_width)
    projected = jnp.dot(flat_normed, qkv_matrix, preferred_element_type=jnp.float32)
    projected = projected.reshape(seqs, length, 3, heads, head_dim) + qkv_bias.astype(jnp.float32)
    cosine_table, sine_table = rotary_tables(length, ROT)
    queries = rotate(projected[:, :, 0], cosine_table, sine_table, ROT, 1.0).astype(jnp.bfloat16)
    key_rows = rotate(projected[:, :, 1], cosine_table, sine_table, ROT, 1.0).astype(jnp.bfloat16)
    value_rows = projected[:, :, 2].astype(jnp.bfloat16)
    context, logsum = lax.map(attend, (queries, key_rows, value_rows))
    flat_ctx = context.reshape(total_rows, local_width)
    pre_act = jnp.dot(flat_normed, in_full, preferred_element_type=jnp.float32) + in_bias.astype(
        jnp.float32
    ).reshape(hidden_units)
    activated, slopes = gelu_parts(pre_act)
    hidden = activated.astype(jnp.bfloat16)
    branch = jnp.dot(flat_ctx, out_full, preferred_element_type=jnp.float32) + jnp.dot(
        hidden, down_full, preferred_element_type=jnp.float32
    )
    summed = lax.psum_scatter(
        branch.reshape(seqs, length, model), "tensor", scatter_dimension=1, tiled=True
    )
    outputs = (input_full + summed + biases[0] + biases[1]).astype(jnp.bfloat16)
    cot_rows = lax.all_gather(cotangent, "tensor", axis=1, tiled=True)
    flat_cot = cot_rows.reshape(total_rows, model)
    backward_weights = (
        lax.all_gather(w_qkv, "dp", axis=0, tiled=True),
        lax.all_gather(b_qkv, "dp", axis=2, tiled=True),
        lax.all_gather(w_out, "dp", axis=1, tiled=True),
        lax.all_gather(w_in, "dp", axis=0, tiled=True),
        lax.all_gather(b_in, "dp", axis=1, tiled=True),
        lax.all_gather(w_down, "dp", axis=1, tiled=True),
    )
    qkv_back, bias_back, out_back, in_back, in_bias_back, down_back = backward_weights
    left_dims = (((0,), (0,)), ((), ()))
    right_dims = (((1,), (1,)), ((), ()))
    grad_down = lax.dot_general(hidden, flat_cot, left_dims, preferred_element_type=jnp.float32)
    pre_grad = (
        lax.dot_general(flat_cot, down_back, right_dims, preferred_element_type=jnp.float32)
        * slopes
    )
    pre_low = pre_grad.astype(jnp.bfloat16)
    grad_in = lax.dot_general(flat_normed, pre_low, left_dims, preferred_element_type=jnp.float32)
    grad_in_bias = jnp.sum(pre_grad, axis=0).reshape(in_bias_back.shape)
    grad_out = lax.dot_general(flat_ctx, flat_cot, left_dims, preferred_element_type=jnp.float32)
    ctx_grad = lax.dot_general(flat_cot, out_back, right_dims, preferred_element_type=jnp.float32)
    ctx_grad = ctx_grad.astype(jnp.bfloat16).reshape(seqs, length, heads, head_dim)
    query_grad, key_grad, value_grad = lax.map(
        attend_back, (queries, key_rows, value_rows, logsum, ctx_grad)
    )
    proj_grad = jnp.stack(
        [
            rotate(query_grad, cosine_table, sine_table, ROT, -1.0),
            rotate(key_grad, cosine_table, sine_table, ROT, -1.0),
            value_grad,
        ],
        axis=2,
    )
    grad_qkv_bias = jnp.sum(proj_grad, axis=(0, 1))
    proj_low = proj_grad.astype(jnp.bfloat16).reshape(total_rows, 3 * local_width)
    grad_qkv = lax.dot_general(flat_normed, proj_low, left_dims, preferred_element_type=jnp.float32)
    grad_qkv = grad_qkv.reshape(model, 3, local_width)
    qkv_back_matrix = qkv_back.reshape(model, 3 * local_width)
    norm_grad = lax.dot_general(
        proj_low, qkv_back_matrix, right_dims, preferred_element_type=jnp.float32
    )
    norm_grad = norm_grad + lax.dot_general(
        pre_low, in_back, right_dims, preferred_element_type=jnp.float32
    )
    own_grad = lax.psum_scatter(
        norm_grad.reshape(seqs, length, model), "tensor", scatter_dimension=1, tiled=True
    )
    unit_grad = own_grad * gain
    cot_full = cotangent.astype(jnp.float32)
    input_grad = cot_full + inv_sigma * (
        unit_grad
        - jnp.mean(unit_grad, axis=-1, keepdims=True)
        - unit_rows * jnp.mean(unit_grad * unit_rows, axis=-1, keepdims=True)
    )
    input_grad = input_grad.astype(jnp.bfloat16)
    gain_part = jnp.sum(own_grad * unit_rows, axis=(0, 1))
    shift_part = jnp.sum(own_grad, axis=(0, 1))
    bias_part = jnp.sum(cot_full, axis=(0, 1))
    bias_pair = jnp.stack([bias_part, bias_part])
    gain_grad, shift_grad, bias_grad = (
        lax.psum_scatter(gain_part, ("dp", "tensor"), scatter_dimension=0, tiled=True),
        lax.psum_scatter(shift_part, ("dp", "tensor"), scatter_dimension=0, tiled=True),
        lax.psum_scatter(bias_pair, ("dp", "tensor"), scatter_dimension=1, tiled=True),
    )
    qkv_grad_out, qkv_bias_grad_out, out_grad_out, in_grad_out, in_bias_grad_out, down_grad_out = (
        lax.psum_scatter(grad_qkv, "dp", scatter_dimension=0, tiled=True),
        lax.psum_scatter(grad_qkv_bias, "dp", scatter_dimension=2, tiled=True),
        lax.psum_scatter(grad_out, "dp", scatter_dimension=1, tiled=True),
        lax.psum_scatter(grad_in, "dp", scatter_dimension=0, tiled=True),
        lax.psum_scatter(grad_in_bias, "dp", scatter_dimension=1, tiled=True),
        lax.psum_scatter(grad_down, "dp", scatter_dimension=1, tiled=True),
    )
    return (
        outputs,
        input_grad,
        gain_grad,
        shift_grad,
        qkv_grad_out,
        qkv_bias_grad_out,
        out_grad_out,
        in_grad_out,
        in_bias_grad_out,
        down_grad_out,
        bias_grad,
    )


def solution(mesh):
    placed = (
        P("dp", "tensor", None),
        P(("dp", "tensor")),
        P(("dp", "tensor")),
        P("dp", None, "tensor"),
        P(None, "tensor", "dp"),
        P("tensor", "dp"),
        P("dp", "tensor"),
        P("tensor", "dp"),
        P("tensor", "dp"),
        P(None, ("dp", "tensor")),
        P("dp", "tensor", None),
    )
    return jax.shard_map(
        body,
        mesh=mesh,
        in_specs=placed,
        out_specs=(
            P("dp", "tensor", None),
            P("dp", "tensor", None),
            P(("dp", "tensor")),
            P(("dp", "tensor")),
            P("dp", None, "tensor"),
            P(None, "tensor", "dp"),
            P("tensor", "dp"),
            P("dp", "tensor"),
            P("tensor", "dp"),
            P("tensor", "dp"),
            P(None, ("dp", "tensor")),
        ),
        check_vma=False,
    )
```

profile of v0, /device:TPU:0, one launch (start us, length us, event | category | flops | bytes accessed | tf_op | source)
XLA Modules:
  0.0 593.6 jit_solution(9107140524121547792)
XLA Ops:
  11.3 42.0 %all-reduce.7 = (f32[768]{0:T(1024)S(1)}, f32[768]{0:T(1024)S(1)}) all-reduce(f32[768]{0:T(1024)S(1)} %dynamic-update-slice.1, f32[768]{0:T(1024)S(1)} %dynamic-update-slice), channel_id=1, replica_groups=mesh['dp'=8,'tensor'=4] {'dp','tensor'}, use_global_device_ids=true, to_apply=%add.1 | all-reduce | flops 1536 | bytes 12288
  58.7 12.8 %all_gather.40 = bf16[768,3,192]{2,1,0:T(4,128)(2,1)S(1)} all-gather(bf16[96,3,192]{2,1,0:T(4,128)(2,1)S(1)} %copy.40), channel_id=1, replica_groups=mesh['dp'=8,'tensor'=4] {'dp'}, dimensions={0}, use_global_device_ids=true | all-gather | bytes 995328 | tf_op jit(solution)/shard_map/all_gather | solution.py:124
  72.6 9.4 %all_gather.41 = bf16[3,3,64]{1,0,2:T(4,128)(2,1)S(1)} all-gather(bf16[3,3,8]{1,0,2:T(4,128)(2,1)S(1)} %copy.42), channel_id=1, replica_groups=mesh['dp'=8,'tensor'=4] {'dp'}, dimensions={2}, use_global_device_ids=true | all-gather | bytes 1296 | tf_op jit(solution)/shard_map/all_gather | solution.py:125
  82.2 8.4 %all_gather.42 = bf16[192,768]{0,1:T(8,128)(2,1)S(1)} all-gather(bf16[192,96]{0,1:T(8,128)(2,1)S(1)} %copy.45), channel_id=1, replica_groups=mesh['dp'=8,'tensor'=4] {'dp'}, dimensions={1}, use_global_device_ids=true | all-gather | bytes 331776 | tf_op jit(solution)/shard_map/all_gather | solution.py:126
  90.6 9.0 %all-gather = bf16[8,16,6]{1,2,0:T(8,128)(2,1)S(1)} all-gather(bf16[1,16,6]{1,2,0:T(8,128)(2,1)S(1)} %bitcast.195), channel_id=1, replica_groups=mesh['dp'=8,'tensor'=4] {'dp'}, dimensions={0}, use_global_device_ids=true | all-gather | bytes 1728 | tf_op jit(solution)/shard_map/all_gather | solution.py:128
  103.7 18.3 %while.47 = (s32[]{:T(128)}, bf16[2,512,3,64]{1,3,2,0:T(8,128)(2,1)S(1)}, f32[2,3,512]{2,1,0:T(4,128)S(1)}, s32[2]{0:T(128)S(1)}, bf16[1024,3,64]{0,2,1:T(8,128)...) while((s32[]{:T(128)}, ...), condition=%wide.region_5.6_spmd, body=%wide.region_2.5_spmd.sunk | while | flops 422149120 | bytes 22214820 | solution.py:74
  122.0 7.9 %all-gather.13.cloned.1.call-done = bf16[1,1024,768]{2,1,0:T(8,128)(2,1)} async-done(((bf16[1,256,768]{2,1,0:T(8,128)(2,1)}), bf16[1,1024,768]{2,1,0:T(8,128)(2,1)}) %all-gather.13.cloned.1.call-update) | async-done | bytes 1572880 | tf_op jit(solution)/shard_map/all_gather | solution.py:168
  132.0 105.2 %while.48 = (s32[]{:T(128)}, f32[1024,3,64]{0,2,1:T(8,128)}, f32[1024,3,64]{0,2,1:T(8,128)}, f32[2,512,3,64]{1,0,3,2:T(2,128)}, s32[2]{0:T(128)S(1)}, /*index=5*...) while((s32[]{:T(128)}, f32[1024,3,64]{0,2,1:T(8,128)}, ...), condition=%wide.region_9.10_spmd.clone, body=%wide.region_7.9_spmd.clone.sunk | while | flops 1048843776 | bytes 72661312 | solution.py:111
  133.7 3.7 fusion.191
  137.4 3.7 fusion.190
  143.4 12.7 %fusion.194 = f32[1,512,3,64]{1,3,2,0:T(8,128)S(1)} fusion(bf16[1024,3,64]{0,2,1:T(8,128)(2,1)S(1)} %get-tuple-element.435, f32[3,512,1024]{2,1,0:T(8,128)} %fusion.190, f32[3,512,1024]{2,1,0:T(8,128)} %fusion.191, f32[3,512]{1,0:T(4,128)S(1)} %dynamic-slice_bitcast_fusion.2, pred[512,1024]{1,0:T(8,128)(4,1)S(1)} %iota_compare_fusion.5), kind=kOutput, calls=%fused_computation.40.clone.1 | convolution fusion | flops 218630656 | bytes 13899776 | tf_op jit(solution)/shard_map/while/body/eval_jaxpr/while/body/eval_jaxpr/hqk,khd->qhd/dot_general | solution.py:102
  156.5 8.1 %dynamic_update_slice.33 = f32[2,512,3,64]{1,0,3,2:T(2,128)} dynamic-update-slice(f32[2,512,3,64]{1,0,3,2:T(2,128)} %get-tuple-element.417, f32[1,512,3,64]{1,0,3,2:T(1,128)S(1)} %copy.75, s32[]{:T(128)} %get-tuple-element.414, s32[]{:T(128)} %constant.78.clone.1..sunk.1, s32[]{:T(128)} %constant.78.clone.1..sunk.1, s32[]{:T(128)} %constant.78.clone.1..sunk.1) | dynamic-update-slice | bytes 786436 | tf_op jit(solution)/shard_map/while/body/eval_jaxpr/while/body/jit(dynamic_update_index_in_dim)/dynamic_update_slice | solution.py:111
  164.6 14.4 %fusion.192 = f32[1024,3,64]{0,2,1:T(8,128)} fusion(f32[3,512,1024]{2,1,0:T(8,128)} %fusion.190, f32[3,512,1024]{2,1,0:T(8,128)} %fusion.191, f32[3,512]{1,0:T(4,128)S(1)} %dynamic-slice_bitcast_fusion.2, pred[512,1024]{1,0:T(8,128)(4,1)S(1)} %iota_compare_fusion.5, f32[1024,3,64]{0,2,1:T(8,128)} %get-tuple-element.415, pred[]{:T(512)S(6)} %compare.3, ...), kind=kOutput, calls=%fused_computation.38.clone.1 | convolution fusion | flops 219023872 | bytes 28000260 | tf_op jit(solution)/shard_map/while/body/eval_jaxpr/while/body/eval_jaxpr/hqk,qhd->khd/dot_general | solution.py:105
  179.1 4.7 fusion.193
  185.9 3.7 fusion.191
  189.6 3.7 fusion.190
  195.6 12.7 %fusion.194 = f32[1,512,3,64]{1,3,2,0:T(8,128)S(1)} fusion(bf16[1024,3,64]{0,2,1:T(8,128)(2,1)S(1)} %get-tuple-element.435, f32[3,512,1024]{2,1,0:T(8,128)} %fusion.190, f32[3,512,1024]{2,1,0:T(8,128)} %fusion.191, f32[3,512]{1,0:T(4,128)S(1)} %dynamic-slice_bitcast_fusion.2, pred[512,1024]{1,0:T(8,128)(4,1)S(1)} %iota_compare_fusion.5), kind=kOutput, calls=%fused_computation.40.clone.1 | convolution fusion | flops 218630656 | bytes 13899776 | tf_op jit(solution)/shard_map/while/body/eval_jaxpr/while/body/eval_jaxpr/hqk,khd->qhd/dot_general | solution.py:102
  208.7 8.1 %dynamic_update_slice.33 = f32[2,512,3,64]{1,0,3,2:T(2,128)} dynamic-update-slice(f32[2,512,3,64]{1,0,3,2:T(2,128)} %get-tuple-element.417, f32[1,512,3,64]{1,0,3,2:T(1,128)S(1)} %copy.75, s32[]{:T(128)} %get-tuple-element.414, s32[]{:T(128)} %constant.78.clone.1..sunk.1, s32[]{:T(128)} %constant.78.clone.1..sunk.1, s32[]{:T(128)} %constant.78.clone.1..sunk.1) | dynamic-update-slice | bytes 786436 | tf_op jit(solution)/shard_map/while/body/eval_jaxpr/while/body/jit(dynamic_update_index_in_dim)/dynamic_update_slice | solution.py:111
  216.8 14.6 %fusion.192 = f32[1024,3,64]{0,2,1:T(8,128)} fusion(f32[3,512,1024]{2,1,0:T(8,128)} %fusion.190, f32[3,512,1024]{2,1,0:T(8,128)} %fusion.191, f32[3,512]{1,0:T(4,128)S(1)} %dynamic-slice_bitcast_fusion.2, pred[512,1024]{1,0:T(8,128)(4,1)S(1)} %iota_compare_fusion.5, f32[1024,3,64]{0,2,1:T(8,128)} %get-tuple-element.415, pred[]{:T(512)S(6)} %compare.3, ...), kind=kOutput, calls=%fused_computation.38.clone.1 | convolution fusion | flops 219023872 | bytes 28000260 | tf_op jit(solution)/shard_map/while/body/eval_jaxpr/while/body/eval_jaxpr/hqk,qhd->khd/dot_general | solution.py:105
  231.4 4.7 fusion.193
  240.5 5.5 multiply_convert_fusion.1
  246.0 4.9 fusion.132
  272.3 4.6 fusion.85
  277.2 4.8 fusion.97
  282.1 4.3 fusion.88
  286.5 67.6 %all-gather.1 = f32[32,24,2]{1,2,0:T(2,128)S(1)} all-gather(f32[1,24,2]{1,2,0:T(2,128)S(1)} %bitcast.196), channel_id=1, replica_groups=mesh['dp'=8,'tensor'=4] {'dp','tensor'}, dimensions={0}, use_global_device_ids=true | all-gather | bytes 6336 | tf_op jit(solution)/shard_map/all_gather | solution.py:121
  356.8 12.5 %all-reduce.4 = f32[3,3,64]{2,1,0:T(4,128)S(1)} all-reduce(f32[3,3,64]{2,1,0:T(4,128)S(1)} %fusion.83), channel_id=7, replica_groups=mesh['dp'=8,'tensor'=4] {'dp'}, use_global_device_ids=true, to_apply=%region_19.20.clone | all-reduce | flops 576 | bytes 4608
  373.0 12.4 %reduce-scatter.16.cloned.1.call-done = f32[1,256,768]{2,1,0:T(8,128)} async-done(((f32[1,1024,768]{2,1,0:T(8,128)}), f32[1,256,768]{2,1,0:T(8,128)}) %reduce-scatter.16.cloned.1.call-update) | async-done | bytes 786448 | tf_op jit(solution)/shard_map/reduce_scatter | solution.py:214
  386.9 61.0 %reduce-scatter.14.cloned.1.call-done = f32[1,256,768]{2,1,0:T(8,128)} async-done(((f32[1,1024,768]{2,1,0:T(8,128)}), f32[1,256,768]{2,1,0:T(8,128)}) %reduce-scatter.14.cloned.1.call-update) | async-done | bytes 786448 | tf_op jit(solution)/shard_map/reduce_scatter | solution.py:164
  450.6 40.4 %all-reduce.6 = (f32[768]{0:T(1024)S(1)}, f32[768]{0:T(1024)S(1)}, f32[2,768]{1,0:T(2,128)S(1)}) all-reduce(f32[768]{0:T(1024)S(1)} %get-tuple-element.186, f32[768]{0:T(1024)S(1)} %get-tuple-element.189, f32[2,768]{1,0:T(2,128)S(1)} %pad_maximum_fusion.3), channel_id=4, replica_groups=mesh['dp'=8,'tensor'=4] {'dp','tensor'}, use_global_device_ids=true, to_apply=%region_14.15.clone | all-reduce | flops 3072 | bytes 24576
  494.3 46.2 %reduce-scatter.20.cloned.1.call-done = f32[96,768]{1,0:T(8,128)} async-done(((f32[768,768]{1,0:T(8,128)}), f32[96,768]{1,0:T(8,128)}) %reduce-scatter.20.cloned.1.call-update) | async-done | bytes 294928 | tf_op jit(solution)/shard_map/reduce_scatter | solution.py:238
  540.5 46.3 %reduce-scatter.22.cloned.1.call-done = f32[768,96]{0,1:T(8,128)} async-done(((f32[768,768]{0,1:T(8,128)}), f32[768,96]{0,1:T(8,128)}) %reduce-scatter.22.cloned.1.call-update) | async-done | bytes 294928 | tf_op jit(solution)/shard_map/reduce_scatter | solution.py:240
  (177 shorter events, 73.5 us)
Async XLA Ops:
  7.2 93.4 %all-gather.7.cloned.1.call-start = ((), (), s32[]{:S(2)}) async-start(), calls=%async_computation.7 | async-start | bytes 1966080 | tf_op jit(solution)/shard_map/all_gather | solution.py:142
  8.4 49.3 %copy-start.17 = (f32[256]{0:T(256)}, f32[256]{0:T(256)S(1)}, u32[]{:S(2)}) copy-start(f32[256]{0:T(256)S(1)} %broadcast_multiply_fusion.3) | copy-start | bytes 3076
  9.6 48.0 %copy-start.19 = (f32[256]{0:T(256)}, f32[256]{0:T(256)S(1)}, u32[]{:S(2)}) copy-start(f32[256]{0:T(256)S(1)} %add_rsqrt_fusion) | copy-start | bytes 3076
  53.4 4.3 copy-start.15
  53.4 19.0 %copy-start.21 = (bf16[3,3,8]{2,1,0:T(4,128)(2,1)S(1)}, bf16[3,3,8]{2,1,0:T(4,128)(2,1)}, u32[]{:S(2)}) copy-start(bf16[3,3,8]{2,1,0:T(4,128)(2,1)} %param.19) | copy-start | bytes 436
  53.4 28.6 %copy-start.14 = (bf16[192,96]{1,0:T(8,128)(2,1)S(1)}, bf16[192,96]{1,0:T(8,128)(2,1)}, u32[]{:S(2)}) copy-start(bf16[192,96]{1,0:T(8,128)(2,1)} %param.20) | copy-start | bytes 110596
  55.4 35.2 %copy-start.22 = (bf16[6,16]{1,0:T(8,128)(2,1)S(1)}, bf16[6,16]{1,0:T(8,128)(2,1)}, u32[]{:S(2)}) copy-start(bf16[6,16]{1,0:T(8,128)(2,1)} %param.22) | copy-start | bytes 580
  55.4 74.4 %all-gather.13.cloned.1.call-start = ((), (), s32[]{:S(2)}) async-start(), calls=%async_computation.11 | async-start | bytes 1966080 | tf_op jit(solution)/shard_map/all_gather | solution.py:168
  56.2 184.3 %all-gather.9.cloned.1.call-start = ((), (), s32[]{:S(2)}) async-start(), calls=%async_computation.8 | async-start | bytes 1327104 | tf_op jit(solution)/shard_map/all_gather | solution.py:127
  56.9 189.0 %all-gather.11.cloned.1.call-start = ((), (), s32[]{:S(2)}) async-start(), calls=%async_computation.9 | async-start | bytes 1327104 | tf_op jit(solution)/shard_map/all_gather | solution.py:129
  57.5 312.5 %reduce-scatter.26.cloned.1.call-start = ((), (), s32[]{:S(2)}) async-start(), calls=%async_computation.17 | async-start | bytes 73728
  72.4 30.8 %copy-start.8 = (bf16[768,3,192]{0,2,1:T(8,128)(2,1)}, bf16[768,3,192]{0,2,1:T(8,128)(2,1)S(1)}, u32[]{:S(2)}) copy-start(bf16[768,3,192]{0,2,1:T(8,128)(2,1)S(1)} %copy.41) | copy-start | bytes 2654212
  122.0 10.0 %copy-start.10 = (bf16[2,512,3,64]{1,3,2,0:T(8,128)(2,1)}, bf16[2,512,3,64]{1,3,2,0:T(8,128)(2,1)S(1)}, u32[]{:S(2)}) copy-start(bf16[2,512,3,64]{1,3,2,0:T(8,128)(2,1)S(1)} %get-tuple-element.148) | copy-start | bytes 1179652
  164.6 14.4 %copy-start.4 = (f32[1024,3,64]{0,2,1:T(8,128)S(1)}, f32[1024,3,64]{0,2,1:T(8,128)}, u32[]{:S(2)}) copy-start(f32[1024,3,64]{0,2,1:T(8,128)} %get-tuple-element.416) | copy-start | bytes 2359300 | tf_op jit(solution)/shard_map/while/body/eval_jaxpr/while
  216.8 14.6 %copy-start.4 = (f32[1024,3,64]{0,2,1:T(8,128)S(1)}, f32[1024,3,64]{0,2,1:T(8,128)}, u32[]{:S(2)}) copy-start(f32[1024,3,64]{0,2,1:T(8,128)} %get-tuple-element.416) | copy-start | bytes 2359300 | tf_op jit(solution)/shard_map/while/body/eval_jaxpr/while
  240.4 11.3 %copy-start.2 = (bf16[24,8,2,512]{3,1,2,0:T(8,128)(2,1)}, bf16[24,8,2,512]{3,1,2,0:T(8,128)(2,1)S(1)}, u32[]{:S(2)}) copy-start(bf16[24,8,2,512]{3,1,2,0:T(8,128)(2,1)S(1)} %copy.72) | copy-start | bytes 1179652
  240.5 5.5 copy-start.1
  246.0 7.4 %copy-start.12 = (f32[1024,8]{0,1:T(8,128)S(1)}, f32[1024,8]{0,1:T(8,128)}, u32[]{:S(2)}) copy-start(f32[1024,8]{0,1:T(8,128)} %copy-done.11) | copy-start | bytes 98308
  246.0 7.4 %copy-start.13 = (f32[1024,8]{0,1:T(8,128)S(1)}, f32[1024,8]{0,1:T(8,128)}, u32[]{:S(2)}) copy-start(f32[1024,8]{0,1:T(8,128)} %get-tuple-element.250) | copy-start | bytes 98308
  251.7 119.6 %reduce-scatter.24.cloned.1.call-start = ((), (), s32[]{:S(2)}) async-start(), calls=%async_computation.16 | async-start | bytes 884736
  257.9 127.5 %reduce-scatter.16.cloned.1.call-start = ((), (), s32[]{:S(2)}) async-start(), calls=%async_computation.12 | async-start | bytes 3932160 | tf_op jit(solution)/shard_map/reduce_scatter | solution.py:214
  266.6 181.4 %reduce-scatter.14.cloned.1.call-start = ((), (), s32[]{:S(2)}) async-start(), calls=%async_computation.10 | async-start | bytes 3932160 | tf_op jit(solution)/shard_map/reduce_scatter | solution.py:164
  272.3 222.1 %reduce-scatter.18.cloned.1.call-start = ((), (), s32[]{:S(2)}) async-start(), calls=%async_computation.13 | async-start | bytes 2654208 | tf_op jit(solution)/shard_map/reduce_scatter | solution.py:235
  276.9 263.6 %reduce-scatter.20.cloned.1.call-start = ((), (), s32[]{:S(2)}) async-start(), calls=%async_computation.14 | async-start | bytes 2654208 | tf_op jit(solution)/shard_map/reduce_scatter | solution.py:238
  282.0 4.5 copy-start.23
  282.0 72.1 %copy-start.25 = (u32[32]{0:T(128)S(1)}, u32[32]{0:T(128)}, u32[]{:S(2)}) copy-start(u32[32]{0:T(128)} %constant.134) | copy-start | bytes 388
  282.1 304.8 %reduce-scatter.22.cloned.1.call-start = ((), (), s32[]{:S(2)}) async-start(), calls=%async_computation.15 | async-start | bytes 2654208 | tf_op jit(solution)/shard_map/reduce_scatter | solution.py:240
  286.4 98.9 %copy-start = (bf16[1,256,768]{2,1,0:T(8,128)(2,1)S(1)}, bf16[1,256,768]{2,1,0:T(8,128)(2,1)}, u32[]{:S(2)}) copy-start(bf16[1,256,768]{2,1,0:T(8,128)(2,1)} %param.15) | copy-start | bytes 1179652
  286.4 98.9 %copy-start.16 = (f32[768]{0:T(1024)S(1)}, f32[768]{0:T(1024)}, u32[]{:S(2)}) copy-start(f32[768]{0:T(1024)} %copy-done.15) | copy-start | bytes 9220
  286.5 98.9 %copy-start.18 = (f32[256]{0:T(256)S(1)}, f32[256]{0:T(256)}, u32[]{:S(2)}) copy-start(f32[256]{0:T(256)} %copy-done.17) | copy-start | bytes 3076
  286.5 98.9 %copy-start.20 = (f32[256]{0:T(256)S(1)}, f32[256]{0:T(256)}, u32[]{:S(2)}) copy-start(f32[256]{0:T(256)} %copy-done.19) | copy-start | bytes 3076
  286.5 161.5 %copy-start.6 = (bf16[1,256,768]{2,1,0:T(8,128)(2,1)S(1)}, bf16[1,256,768]{2,1,0:T(8,128)(2,1)}, u32[]{:S(2)}) copy-start(bf16[1,256,768]{2,1,0:T(8,128)(2,1)} %param.25) | copy-start | bytes 1179652
  (8 other events, 18.8 us)
Sparse Core Ops, SparseCore 0:
  55.6 36.8 all-gather.6
  94.0 35.8 all-gather.12
  131.8 22.8 all-gather.8
  156.4 23.9 all-gather.10
  251.8 32.6 reduce-scatter.25
  287.5 34.9 reduce-scatter.23
  324.8 60.5 reduce-scatter.15
  387.6 60.2 reduce-scatter.13
  451.9 42.4 reduce-scatter.17
  498.1 42.3 reduce-scatter.19
  544.5 42.3 reduce-scatter.21
where the time goes:
time: 603 us; the launch traced here: 594 us
  blocking collectives  202 us (33%)
  waiting for transfers between devices  177 us (29%)
  matrix products  127 us (21%)
  local copies, waits for them, and re-layouts  38.7 us (6%)
  other arithmetic  22.8 us (4%)
  between operations  15.3 us (3%)
  loops' own time  9.92 us (2%)
    unnamed x3, blocking collectives  95 us
    all_gather x1, blocking collectives, body(): lax.all_gather(out_bias, ('dp', 'tensor'), axis=1, tiled=True)  67.6 us
    reduce_scatter x1, waiting for transfers between devices, body(): lax.psum_scatter(branch.reshape(seqs, length, model), 'tensor', scatter_d...  61 us
    reduce_scatter x1, waiting for transfers between devices, body(): lax.psum_scatter(grad_down, 'dp', scatter_dimension=1, tiled=True)  46.3 us
    reduce_scatter x1, waiting for transfers between devices, body(): lax.psum_scatter(grad_in, 'dp', scatter_dimension=0, tiled=True)  46.2 us
    dot_general x2, matrix products, one_block(): jnp.einsum('hqk,qhd->khd', score_grad, q_rows, preferred_element_type=jnp...  29 us
    dot_general x2, matrix products, one_block(): jnp.einsum('hqk,khd->qhd', score_grad, key_rows, preferred_element_type=j...  25.4 us
    dynamic_update_slice x4, local copies, waits for them, and re-layouts, attend_back(): lax.scan(one_block, (zero_grads, zero_grads), jnp.arange(length // block_...  17 us
  transfers between devices with their start and end apart: 11, of which 6 were waited for; matrix products, arithmetic and copies ran while one was open for 29% of the time, Pallas kernels for 0%

commit v1 on v0

--- a/solution.py
+++ b/solution.py
@@ -9,6 +9,28 @@
 ROOT_HALF = 0.7071067811865476
 INV_ROOT_TAU = 0.3989422804014327
 NEG_BIG = -1e30
+
+
+def joined_along(parts, dim):
+    shape = list(parts.shape[1:])
+    shape[dim] *= parts.shape[0]
+    return jnp.moveaxis(parts, 0, dim).reshape(shape)
+
+
+def doubled(x, axis):
+    size = lax.axis_size(axis)
+    tiles = x[None]
+    for level in range(size.bit_length() - 1):
+        bit = 1 << level
+        other = lax.ppermute(tiles, axis, [(i, i ^ bit) for i in range(size)])
+        both = jnp.stack([tiles, other])
+        upper = lax.axis_index(axis) >> level & 1
+        tiles = jnp.where(upper == 0, both, both[::-1]).reshape(-1, *x.shape)
+    return tiles
+
+
+def collect(x, axis, dim):
+    return joined_along(doubled(x, axis), dim)
 
 
 def rotary_tables(length, rot_dims):
@@ -118,7 +140,7 @@
     gain, shift, biases = (
         lax.all_gather(ln_gain, ("dp", "tensor"), axis=0, tiled=True),
         lax.all_gather(ln_bias, ("dp", "tensor"), axis=0, tiled=True),
-        lax.all_gather(out_bias, ("dp", "tensor"), axis=1, tiled=True),
+        collect(out_bias, ("dp", "tensor"), 1),
     )
     forward_weights = (
         lax.all_gather(w_qkv, "dp", axis=0, tiled=True),

time: 603 us -> 603 us (level)
  blocking collectives: 202 us -> 134 us
  waiting for transfers between devices: 177 us -> 241 us
    all_gather x1 -> x0, blocking collectives: 67.6 us -> none  [body(): lax.all_gather(out_bias, ('dp', 'tensor'), axis=1, tiled=True)]
    reduce_scatter x1, waiting for transfers between devices: 12.4 us -> 61.1 us  [body(): lax.psum_scatter(norm_grad.reshape(seqs, length, model), 'tensor', scatte...]
    ppermute x0 -> x5, waiting for transfers between devices: none -> 10.1 us  [doubled(): other = lax.ppermute(tiles, axis, [(i, i ^ bit) for i in range(size)])]
  transfers between devices with their start and end apart: 11 -> 16, of which waited for: 6 -> 12; matrix products, arithmetic and copies ran while one was open for 29% -> 29% of each run, Pallas kernels for 0% -> 0%
where the time goes in v1:
time: 603 us; the launch traced here: 593 us
  waiting for transfers between devices  241 us (40%)
  blocking collectives  134 us (22%)
  matrix products  127 us (21%)
  local copies, waits for them, and re-layouts  38.6 us (6%)
  other arithmetic  21.7 us (4%)
  between operations  15.4 us (3%)
  loops' own time  9.92 us (2%)
  starting transfers between devices  6.24 us (1%)
    unnamed x3, blocking collectives  94.6 us
    reduce_scatter x1, waiting for transfers between devices, body(): lax.psum_scatter(norm_grad.reshape(seqs, length, model), 'tensor', scatte...  61.1 us
    reduce_scatter x1, waiting for transfers between devices, body(): lax.psum_scatter(branch.reshape(seqs, length, model), 'tensor', scatter_d...  61 us
    reduce_scatter x1, waiting for transfers between devices, body(): lax.psum_scatter(grad_down, 'dp', scatter_dimension=1, tiled=True)  46.3 us
    reduce_scatter x1, waiting for transfers between devices, body(): lax.psum_scatter(grad_in, 'dp', scatter_dimension=0, tiled=True)  46.2 us
    dot_general x2, matrix products, one_block(): jnp.einsum('hqk,qhd->khd', score_grad, q_rows, preferred_element_type=jnp...  29 us
    dot_general x2, matrix products, one_block(): jnp.einsum('hqk,khd->qhd', score_grad, key_rows, preferred_element_type=j...  25.4 us
    dynamic_update_slice x4, local copies, waits for them, and re-layouts, attend_back(): lax.scan(one_block, (zero_grads, zero_grads), jnp.arange(length // block_...  16.9 us
  transfers between devices with their start and end apart: 16, of which 12 were waited for; matrix products, arithmetic and copies ran while one was open for 29% of the time, Pallas kernels for 0%

profile of v1, /device:TPU:0, one launch (start us, length us, event | category | flops | bytes accessed | tf_op | source)
XLA Modules:
  0.0 593.4 jit_solution(8830012395577200691)
XLA Ops:
  11.3 42.0 %all-reduce.7 = (f32[768]{0:T(1024)S(1)}, f32[768]{0:T(1024)S(1)}) all-reduce(f32[768]{0:T(1024)S(1)} %dynamic-update-slice.1, f32[768]{0:T(1024)S(1)} %dynamic-update-slice), channel_id=1, replica_groups=mesh['dp'=8,'tensor'=4] {'dp','tensor'}, use_global_device_ids=true, to_apply=%add.1 | all-reduce | flops 1536 | bytes 12288
  58.7 12.8 %all_gather.37 = bf16[768,3,192]{2,1,0:T(4,128)(2,1)S(1)} all-gather(bf16[96,3,192]{2,1,0:T(4,128)(2,1)S(1)} %copy.42), channel_id=1, replica_groups=mesh['dp'=8,'tensor'=4] {'dp'}, dimensions={0}, use_global_device_ids=true | all-gather | bytes 995328 | tf_op jit(solution)/shard_map/all_gather | solution.py:146
  72.5 9.4 %all_gather.38 = bf16[3,3,64]{1,0,2:T(4,128)(2,1)S(1)} all-gather(bf16[3,3,8]{1,0,2:T(4,128)(2,1)S(1)} %copy.44), channel_id=1, replica_groups=mesh['dp'=8,'tensor'=4] {'dp'}, dimensions={2}, use_global_device_ids=true | all-gather | bytes 1296 | tf_op jit(solution)/shard_map/all_gather | solution.py:147
  82.1 8.4 %all_gather.39 = bf16[192,768]{0,1:T(8,128)(2,1)S(1)} all-gather(bf16[192,96]{0,1:T(8,128)(2,1)S(1)} %copy.47), channel_id=1, replica_groups=mesh['dp'=8,'tensor'=4] {'dp'}, dimensions={1}, use_global_device_ids=true | all-gather | bytes 331776 | tf_op jit(solution)/shard_map/all_gather | solution.py:148
  90.6 9.0 %all-gather = bf16[8,16,6]{1,2,0:T(8,128)(2,1)S(1)} all-gather(bf16[1,16,6]{1,2,0:T(8,128)(2,1)S(1)} %bitcast.221), channel_id=1, replica_groups=mesh['dp'=8,'tensor'=4] {'dp'}, dimensions={0}, use_global_device_ids=true | all-gather | bytes 1728 | tf_op jit(solution)/shard_map/all_gather | solution.py:150
  103.7 18.3 %while.47 = (s32[]{:T(128)}, bf16[2,512,3,64]{1,3,2,0:T(8,128)(2,1)S(1)}, f32[2,3,512]{2,1,0:T(4,128)S(1)}, s32[2]{0:T(128)S(1)}, bf16[1024,3,64]{0,2,1:T(8,128)...) while((s32[]{:T(128)}, ...), condition=%wide.region_5.6_spmd, body=%wide.region_2.5_spmd.sunk | while | flops 422149120 | bytes 22214820 | solution.py:96
  122.0 7.9 %all-gather.12.cloned.1.call-done = bf16[1,1024,768]{2,1,0:T(8,128)(2,1)} async-done(((bf16[1,256,768]{2,1,0:T(8,128)(2,1)}), bf16[1,1024,768]{2,1,0:T(8,128)(2,1)}) %all-gather.12.cloned.1.call-update) | async-done | bytes 1572880 | tf_op jit(solution)/shard_map/all_gather | solution.py:190
  132.0 105.0 %while.48 = (s32[]{:T(128)}, f32[1024,3,64]{0,2,1:T(8,128)}, f32[1024,3,64]{0,2,1:T(8,128)}, f32[2,512,3,64]{1,0,3,2:T(2,128)}, s32[2]{0:T(128)S(1)}, /*index=5*...) while((s32[]{:T(128)}, f32[1024,3,64]{0,2,1:T(8,128)}, ...), condition=%wide.region_9.10_spmd.clone, body=%wide.region_7.9_spmd.clone.sunk | while | flops 1048843776 | bytes 72661312 | solution.py:133
  133.7 3.7 fusion.194
  137.4 3.7 fusion.193
  143.4 12.7 %fusion.197 = f32[1,512,3,64]{1,3,2,0:T(8,128)S(1)} fusion(bf16[1024,3,64]{0,2,1:T(8,128)(2,1)S(1)} %get-tuple-element.439, f32[3,512,1024]{2,1,0:T(8,128)} %fusion.193, f32[3,512,1024]{2,1,0:T(8,128)} %fusion.194, f32[3,512]{1,0:T(4,128)S(1)} %dynamic-slice_bitcast_fusion.2, pred[512,1024]{1,0:T(8,128)(4,1)S(1)} %iota_compare_fusion.5), kind=kOutput, calls=%fused_computation.40.clone.1 | convolution fusion | flops 218630656 | bytes 13899776 | tf_op jit(solution)/shard_map/while/body/eval_jaxpr/while/body/eval_jaxpr/hqk,khd->qhd/dot_general | solution.py:124
  156.5 8.1 %dynamic_update_slice.33 = f32[2,512,3,64]{1,0,3,2:T(2,128)} dynamic-update-slice(f32[2,512,3,64]{1,0,3,2:T(2,128)} %get-tuple-element.421, f32[1,512,3,64]{1,0,3,2:T(1,128)S(1)} %copy.81, s32[]{:T(128)} %get-tuple-element.418, s32[]{:T(128)} %constant.71.clone.1..sunk.1, s32[]{:T(128)} %constant.71.clone.1..sunk.1, s32[]{:T(128)} %constant.71.clone.1..sunk.1) | dynamic-update-slice | bytes 786436 | tf_op jit(solution)/shard_map/while/body/eval_jaxpr/while/body/jit(dynamic_update_index_in_dim)/dynamic_update_slice | solution.py:133
  164.5 14.4 %fusion.195 = f32[1024,3,64]{0,2,1:T(8,128)} fusion(f32[3,512,1024]{2,1,0:T(8,128)} %fusion.193, f32[3,512,1024]{2,1,0:T(8,128)} %fusion.194, f32[3,512]{1,0:T(4,128)S(1)} %dynamic-slice_bitcast_fusion.2, pred[512,1024]{1,0:T(8,128)(4,1)S(1)} %iota_compare_fusion.5, f32[1024,3,64]{0,2,1:T(8,128)} %get-tuple-element.419, pred[]{:T(512)S(6)} %compare.3, ...), kind=kOutput, calls=%fused_computation.38.clone.1 | convolution fusion | flops 219023872 | bytes 28000260 | tf_op jit(solution)/shard_map/while/body/eval_jaxpr/while/body/eval_jaxpr/hqk,qhd->khd/dot_general | solution.py:127
  179.0 4.7 fusion.196
  185.8 3.7 fusion.194
  189.5 3.7 fusion.193
  195.5 12.7 %fusion.197 = f32[1,512,3,64]{1,3,2,0:T(8,128)S(1)} fusion(bf16[1024,3,64]{0,2,1:T(8,128)(2,1)S(1)} %get-tuple-element.439, f32[3,512,1024]{2,1,0:T(8,128)} %fusion.193, f32[3,512,1024]{2,1,0:T(8,128)} %fusion.194, f32[3,512]{1,0:T(4,128)S(1)} %dynamic-slice_bitcast_fusion.2, pred[512,1024]{1,0:T(8,128)(4,1)S(1)} %iota_compare_fusion.5), kind=kOutput, calls=%fused_computation.40.clone.1 | convolution fusion | flops 218630656 | bytes 13899776 | tf_op jit(solution)/shard_map/while/body/eval_jaxpr/while/body/eval_jaxpr/hqk,khd->qhd/dot_general | solution.py:124
  208.6 8.0 %dynamic_update_slice.33 = f32[2,512,3,64]{1,0,3,2:T(2,128)} dynamic-update-slice(f32[2,512,3,64]{1,0,3,2:T(2,128)} %get-tuple-element.421, f32[1,512,3,64]{1,0,3,2:T(1,128)S(1)} %copy.81, s32[]{:T(128)} %get-tuple-element.418, s32[]{:T(128)} %constant.71.clone.1..sunk.1, s32[]{:T(128)} %constant.71.clone.1..sunk.1, s32[]{:T(128)} %constant.71.clone.1..sunk.1) | dynamic-update-slice | bytes 786436 | tf_op jit(solution)/shard_map/while/body/eval_jaxpr/while/body/jit(dynamic_update_index_in_dim)/dynamic_update_slice | solution.py:133
  216.7 14.6 %fusion.195 = f32[1024,3,64]{0,2,1:T(8,128)} fusion(f32[3,512,1024]{2,1,0:T(8,128)} %fusion.193, f32[3,512,1024]{2,1,0:T(8,128)} %fusion.194, f32[3,512]{1,0:T(4,128)S(1)} %dynamic-slice_bitcast_fusion.2, pred[512,1024]{1,0:T(8,128)(4,1)S(1)} %iota_compare_fusion.5, f32[1024,3,64]{0,2,1:T(8,128)} %get-tuple-element.419, pred[]{:T(512)S(6)} %compare.3, ...), kind=kOutput, calls=%fused_computation.38.clone.1 | convolution fusion | flops 219023872 | bytes 28000260 | tf_op jit(solution)/shard_map/while/body/eval_jaxpr/while/body/eval_jaxpr/hqk,qhd->khd/dot_general | solution.py:127
  231.2 4.7 fusion.196
  240.3 5.5 multiply_convert_fusion.1
  245.8 4.9 fusion.135
  272.1 4.7 fusion.85
  277.0 4.8 fusion.97
  281.9 4.3 fusion.88
  303.7 12.1 %all-reduce.4 = f32[3,3,64]{2,1,0:T(4,128)S(1)} all-reduce(f32[3,3,64]{2,1,0:T(4,128)S(1)} %fusion.83), channel_id=7, replica_groups=mesh['dp'=8,'tensor'=4] {'dp'}, use_global_device_ids=true, to_apply=%region_19.20.clone | all-reduce | flops 576 | bytes 4608
  317.9 4.5 reduce-scatter.24.cloned.1.call-done
  324.0 61.1 %reduce-scatter.16.cloned.1.call-done = f32[1,256,768]{2,1,0:T(8,128)} async-done(((f32[1,1024,768]{2,1,0:T(8,128)}), f32[1,256,768]{2,1,0:T(8,128)}) %reduce-scatter.16.cloned.1.call-update) | async-done | bytes 786448 | tf_op jit(solution)/shard_map/reduce_scatter | solution.py:236
  386.7 61.0 %reduce-scatter.14.cloned.1.call-done = f32[1,256,768]{2,1,0:T(8,128)} async-done(((f32[1,1024,768]{2,1,0:T(8,128)}), f32[1,256,768]{2,1,0:T(8,128)}) %reduce-scatter.14.cloned.1.call-update) | async-done | bytes 786448 | tf_op jit(solution)/shard_map/reduce_scatter | solution.py:186
  450.4 40.4 %all-reduce.6 = (f32[768]{0:T(1024)S(1)}, f32[768]{0:T(1024)S(1)}, f32[2,768]{1,0:T(2,128)S(1)}) all-reduce(f32[768]{0:T(1024)S(1)} %get-tuple-element.186, f32[768]{0:T(1024)S(1)} %get-tuple-element.189, f32[2,768]{1,0:T(2,128)S(1)} %pad_maximum_fusion.6), channel_id=4, replica_groups=mesh['dp'=8,'tensor'=4] {'dp','tensor'}, use_global_device_ids=true, to_apply=%region_14.15.clone | all-reduce | flops 3072 | bytes 24576
  494.1 46.2 %reduce-scatter.20.cloned.1.call-done = f32[96,768]{1,0:T(8,128)} async-done(((f32[768,768]{1,0:T(8,128)}), f32[96,768]{1,0:T(8,128)}) %reduce-scatter.20.cloned.1.call-update) | async-done | bytes 294928 | tf_op jit(solution)/shard_map/reduce_scatter | solution.py:260
  540.4 46.3 %reduce-scatter.22.cloned.1.call-done = f32[768,96]{0,1:T(8,128)} async-done(((f32[768,768]{0,1:T(8,128)}), f32[768,96]{0,1:T(8,128)}) %reduce-scatter.22.cloned.1.call-update) | async-done | bytes 294928 | tf_op jit(solution)/shard_map/reduce_scatter | solution.py:262
  (199 shorter events, 88.1 us)
Async XLA Ops:
  7.2 93.4 %all-gather.6.cloned.1.call-start = ((), (), s32[]{:S(2)}) async-start(), calls=%async_computation.7 | async-start | bytes 1966080 | tf_op jit(solution)/shard_map/all_gather | solution.py:164
  8.4 49.3 %copy-start.18 = (f32[256]{0:T(256)}, f32[256]{0:T(256)S(1)}, u32[]{:S(2)}) copy-start(f32[256]{0:T(256)S(1)} %broadcast_multiply_fusion.3) | copy-start | bytes 3076
  9.6 48.0 %copy-start.20 = (f32[256]{0:T(256)}, f32[256]{0:T(256)S(1)}, u32[]{:S(2)}) copy-start(f32[256]{0:T(256)S(1)} %add_rsqrt_fusion) | copy-start | bytes 3076
  53.4 19.0 %copy-start.22 = (bf16[3,3,8]{2,1,0:T(4,128)(2,1)S(1)}, bf16[3,3,8]{2,1,0:T(4,128)(2,1)}, u32[]{:S(2)}) copy-start(bf16[3,3,8]{2,1,0:T(4,128)(2,1)} %param.19) | copy-start | bytes 436
  53.4 28.6 %copy-start.15 = (bf16[192,96]{1,0:T(8,128)(2,1)S(1)}, bf16[192,96]{1,0:T(8,128)(2,1)}, u32[]{:S(2)}) copy-start(bf16[192,96]{1,0:T(8,128)(2,1)} %param.20) | copy-start | bytes 110596
  55.4 35.2 %copy-start.23 = (bf16[6,16]{1,0:T(8,128)(2,1)S(1)}, bf16[6,16]{1,0:T(8,128)(2,1)}, u32[]{:S(2)}) copy-start(bf16[6,16]{1,0:T(8,128)(2,1)} %param.22) | copy-start | bytes 580
  55.4 74.4 %all-gather.12.cloned.1.call-start = ((), (), s32[]{:S(2)}) async-start(), calls=%async_computation.11 | async-start | bytes 1966080 | tf_op jit(solution)/shard_map/all_gather | solution.py:190
  56.2 184.1 %all-gather.8.cloned.1.call-start = ((), (), s32[]{:S(2)}) async-start(), calls=%async_computation.8 | async-start | bytes 1327104 | tf_op jit(solution)/shard_map/all_gather | solution.py:149
  56.9 188.9 %all-gather.10.cloned.1.call-start = ((), (), s32[]{:S(2)}) async-start(), calls=%async_computation.9 | async-start | bytes 1327104 | tf_op jit(solution)/shard_map/all_gather | solution.py:151
  57.5 259.1 %reduce-scatter.26.cloned.1.call-start = ((), (), s32[]{:S(2)}) async-start(), calls=%async_computation.17 | async-start | bytes 73728
  72.4 30.8 %copy-start.9 = (bf16[768,3,192]{0,2,1:T(8,128)(2,1)}, bf16[768,3,192]{0,2,1:T(8,128)(2,1)S(1)}, u32[]{:S(2)}) copy-start(bf16[768,3,192]{0,2,1:T(8,128)(2,1)S(1)} %copy.43) | copy-start | bytes 2654212
  164.5 14.4 %copy-start.4 = (f32[1024,3,64]{0,2,1:T(8,128)S(1)}, f32[1024,3,64]{0,2,1:T(8,128)}, u32[]{:S(2)}) copy-start(f32[1024,3,64]{0,2,1:T(8,128)} %get-tuple-element.420) | copy-start | bytes 2359300 | tf_op jit(solution)/shard_map/while/body/eval_jaxpr/while
  216.7 14.6 %copy-start.4 = (f32[1024,3,64]{0,2,1:T(8,128)S(1)}, f32[1024,3,64]{0,2,1:T(8,128)}, u32[]{:S(2)}) copy-start(f32[1024,3,64]{0,2,1:T(8,128)} %get-tuple-element.420) | copy-start | bytes 2359300 | tf_op jit(solution)/shard_map/while/body/eval_jaxpr/while
  240.2 11.3 %copy-start.2 = (bf16[24,8,2,512]{3,1,2,0:T(8,128)(2,1)}, bf16[24,8,2,512]{3,1,2,0:T(8,128)(2,1)S(1)}, u32[]{:S(2)}) copy-start(bf16[24,8,2,512]{3,1,2,0:T(8,128)(2,1)S(1)} %copy.75) | copy-start | bytes 1179652
  251.5 70.9 %reduce-scatter.24.cloned.1.call-start = ((), (), s32[]{:S(2)}) async-start(), calls=%async_computation.16 | async-start | bytes 884736
  257.7 127.4 %reduce-scatter.16.cloned.1.call-start = ((), (), s32[]{:S(2)}) async-start(), calls=%async_computation.12 | async-start | bytes 3932160 | tf_op jit(solution)/shard_map/reduce_scatter | solution.py:236
  266.4 181.4 %reduce-scatter.14.cloned.1.call-start = ((), (), s32[]{:S(2)}) async-start(), calls=%async_computation.10 | async-start | bytes 3932160 | tf_op jit(solution)/shard_map/reduce_scatter | solution.py:186
  272.0 222.1 %reduce-scatter.18.cloned.1.call-start = ((), (), s32[]{:S(2)}) async-start(), calls=%async_computation.13 | async-start | bytes 2654208 | tf_op jit(solution)/shard_map/reduce_scatter | solution.py:257
  276.7 263.6 %reduce-scatter.20.cloned.1.call-start = ((), (), s32[]{:S(2)}) async-start(), calls=%async_computation.14 | async-start | bytes 2654208 | tf_op jit(solution)/shard_map/reduce_scatter | solution.py:260
  281.8 19.3 %copy-start.26 = (u32[32]{0:T(128)S(1)}, u32[32]{0:T(128)}, u32[]{:S(2)}) copy-start(u32[32]{0:T(128)} %constant.151) | copy-start | bytes 388
  281.8 304.8 %reduce-scatter.22.cloned.1.call-start = ((), (), s32[]{:S(2)}) async-start(), calls=%async_computation.15 | async-start | bytes 2654208 | tf_op jit(solution)/shard_map/reduce_scatter | solution.py:262
  286.2 17.3 %copy-start.6 = (f32[1024,3,64]{0,2,1:T(8,128)S(1)}, f32[1024,3,64]{0,2,1:T(8,128)}, u32[]{:S(2)}) copy-start(f32[1024,3,64]{0,2,1:T(8,128)} %get-tuple-element.152) | copy-start | bytes 2359300
  286.2 98.9 %copy-start = (bf16[1,256,768]{2,1,0:T(8,128)(2,1)S(1)}, bf16[1,256,768]{2,1,0:T(8,128)(2,1)}, u32[]{:S(2)}) copy-start(bf16[1,256,768]{2,1,0:T(8,128)(2,1)} %param.15) | copy-start | bytes 1179652
  286.2 98.9 %copy-start.17 = (f32[768]{0:T(1024)S(1)}, f32[768]{0:T(1024)}, u32[]{:S(2)}) copy-start(f32[768]{0:T(1024)} %copy-done.16) | copy-start | bytes 9220
  286.2 98.9 %copy-start.19 = (f32[256]{0:T(256)S(1)}, f32[256]{0:T(256)}, u32[]{:S(2)}) copy-start(f32[256]{0:T(256)} %copy-done.18) | copy-start | bytes 3076
  286.2 98.9 %copy-start.21 = (f32[256]{0:T(256)S(1)}, f32[256]{0:T(256)}, u32[]{:S(2)}) copy-start(f32[256]{0:T(256)} %copy-done.20) | copy-start | bytes 3076
  286.3 161.5 %copy-start.7 = (bf16[1,256,768]{2,1,0:T(8,128)(2,1)S(1)}, bf16[1,256,768]{2,1,0:T(8,128)(2,1)}, u32[]{:S(2)}) copy-start(bf16[1,256,768]{2,1,0:T(8,128)(2,1)} %param.25) | copy-start | bytes 1179652
  286.3 3.6 collective-permute-start
  290.0 4.5 collective-permute-start.1
  294.5 1.2 collective-permute-start.2
  295.8 3.7 collective-permute-start.3
  299.5 3.8 collective-permute-start.4
  (14 other events, 57.9 us)
Sparse Core Ops, SparseCore 0:
  55.6 36.8 all-gather.5
  94.0 35.8 all-gather.11
  131.8 22.8 all-gather.7
  156.4 24.0 all-gather.9
  251.6 32.5 reduce-scatter.25
  287.2 35.0 reduce-scatter.23
  324.7 60.4 reduce-scatter.15
  387.4 60.2 reduce-scatter.13
  451.7 42.3 reduce-scatter.17
  497.9 42.4 reduce-scatter.19
  544.3 42.3 reduce-scatter.21
